TPU v7x, 32 devices: a whole 2x2x4 slice. The times are simulated.
32 devices in a mesh: real: 2 (over x), tile: 16 (over z, y, core).
Axes of the slice: x: 2, y: 2, z: 4, core: 2. Of those that a mesh axis runs over, the one named last changes fastest.
Arguments:
- positions: float32 [6, 8192], P('real', 'tile'), parts along dimension 0, may hold values from -1.5 to 125.5, as said below
- residual: float32 [6, 8192], P('real', 'tile'), parts along dimension 0, may hold values from -24 to 24
- iterate: float32 [6, 8192], P('real', 'tile'), parts along dimension 0, may hold values from -6 to 6
Outputs:
- new_iterate: float32 [6, 8192], P('real', 'tile'), parts along dimension 0
- new_residual: float32 [6, 8192], P('real', 'tile'), parts along dimension 0
- new_direction: float32 [6, 8192], P('real', 'tile'), parts along dimension 0
There are 2 independent parts, one for each index of `real`. A program takes and returns all parts, laid end to end along the dimension named above; each array names one. Nothing has to cross between parts.
Inputs may be any that keep to these rules, and one draw needn't show every extreme that they name: `positions`: distinct blobs are at least 1 apart.
All inputs are finite; a program needn't handle non-finite values.
Results may differ from a plain program's by a relative error of at most 0.0003.
Values sent between devices are 32-bit elements; how exact they have to be, the bound alone decides.
A program may use at most 64 MiB of HBM per device.

v0:
```python
import jax
import jax.numpy as jnp
from jax import lax
from jax.sharding import PartitionSpec as P


def pair_terms(row_pos, col_pos):
    separation = row_pos[:, :, None] - col_pos[:, None, :]
    squared = jnp.sum(separation * separation, axis=0)
    radius = jnp.sqrt(squared)
    inverse = 1.0 / jnp.maximum(radius, 0.5)
    inverse_sq = inverse * inverse
    far_scalar = 0.75 * inverse * (1.0 + 2.0 / 3.0 * inverse_sq)
    far_tensor = 0.75 * (1.0 - 2.0 * inverse_sq) * inverse_sq * inverse
    touching = radius < 2.0
    scalar_part = jnp.where(touching, 1.0 - 9.0 / 32.0 * radius, far_scalar)
    tensor_part = jnp.where(touching, 3.0 / 32.0 * inverse, far_tensor)
    return (separation, scalar_part, tensor_part)


def toward_rows(separation, scalar_part, tensor_part, col_forces):
    projected = jnp.sum(separation * col_forces[:, None, :], axis=0)
    return jnp.sum(
        scalar_part[None] * col_forces[:, None, :] + (tensor_part * projected)[None] * separation,
        axis=2,
    )


def shards(positions, residual, iterate):
    own_blobs = positions.shape[1]
    old_norm = lax.psum(jnp.sum(residual * residual), "tile")
    col_pos = lax.all_gather(positions, "tile", axis=1, tiled=True)
    col_forces = lax.all_gather(residual, "tile", axis=1, tiled=True)
    portion_cols = col_pos.shape[1]
    col_block = portion_cols
    for factor in (4, 2, 1):
        col_block = factor * own_blobs
        break

    def add_block(turn_index, running):
        block_pos = lax.dynamic_slice_in_dim(col_pos, turn_index * col_block, col_block, 1)
        block_forces = lax.dynamic_slice_in_dim(col_forces, turn_index * col_block, col_block, 1)
        separation, scalar_part, tensor_part = pair_terms(positions, block_pos)
        return running + toward_rows(separation, scalar_part, tensor_part, block_forces)

    applied = lax.fori_loop(0, portion_cols // col_block, add_block, jnp.zeros_like(residual))
    curvature = lax.psum(jnp.sum(residual * applied), "tile")
    step_size = old_norm / curvature
    new_residual = residual - step_size * applied
    new_norm = lax.psum(jnp.sum(new_residual * new_residual), "tile")
    new_iterate = iterate + step_size * residual
    new_direction = new_residual + new_norm / old_norm * residual
    return (new_iterate, new_residual, new_direction)


def solution(mesh):
    return jax.shard_map(
        shards,
        mesh=mesh,
        in_specs=(P("real", "tile"), P("real", "tile"), P("real", "tile")),
        out_specs=(P("real", "tile"), P("real", "tile"), P("real", "tile")),
        check_vma=False,
    )
```

profile of v0, /device:TPU:0, one launch (start us, length us, event | category | flops | bytes accessed | tf_op | source)
XLA Modules:
  0.0 165.1 jit_solution(6442482215898881509)
XLA Ops:
  0.6 23.7 %all_gather.6 = f32[3,8192]{1,0:T(4,128)S(1)} all-gather(f32[3,512]{1,0:T(4,128)} %param.5), channel_id=1, replica_groups=mesh['real'=2,'tile'=16] {'tile'}, dimensions={1}, use_global_device_ids=true | all-gather | bytes 104448 | tf_op jit(solution)/shard_map/all_gather | solution.py:32
  24.3 18.0 %all_gather.7 = f32[3,8192]{1,0:T(4,128)S(1)} all-gather(f32[3,512]{1,0:T(4,128)} %param.6), channel_id=1, replica_groups=mesh['real'=2,'tile'=16] {'tile'}, dimensions={1}, use_global_device_ids=true | all-gather | bytes 104448 | tf_op jit(solution)/shard_map/all_gather | solution.py:33
  42.4 0.0 copy-start.1
  42.4 0.0 copy-start.3
  42.4 56.4 %while.14 = (s32[]{:T(128)}, f32[3,512]{1,0:T(4,128)S(1)}, f32[3,512]{1,0:T(4,128)}, f32[3,8192]{1,0:T(4,128)S(1)}, f32[3,8192]{1,0:T(4,128)S(1)}, /*index=5*/s32[]{:T(128)}, s32[]{:T(128)}, s32[]{:T(128)}, s32[]{:T(128)}) while((s32[]{:T(128)}, f32[3,512]{1,0:T(4,128)S(1)}, f32[3,512]{1,0:T(4,128)}, f32[3,8192]{1,0:T(4,128)S(1)}, ...), condition=%wide.region_6.7_spmd.clone, body=%wide.region_2.6_spmd.clone.sunk | while | flops 49284612 | bytes 33812656 | solution.py:46
  42.4 8.2 %fusion.10 = (f32[512,2048]{1,0:T(8,128)S(1)}, f32[512,2048]{1,0:T(8,128)S(1)}) fusion(f32[3,2048]{1,0:T(4,128)S(1)} %get-tuple-element.177, f32[3,512]{1,0:T(4,128)} %get-tuple-element.203, f32[3,2048]{1,0:T(4,128)S(1)} %get-tuple-element.178), kind=kLoop, calls=%fused_computation.3.clone.1 | loop fusion | flops 13631488 | bytes 8443904 | tf_op jit(solution)/shard_map/while/body/eval_jaxpr/reduce_sum | solution.py:9
  50.6 0.0 copy-start
  50.6 3.6 %fusion.11 = (f32[512,2048]{1,0:T(8,128)S(1)}, f32[512,2048]{1,0:T(8,128)S(1)}) fusion(f32[512,2048]{1,0:T(8,128)S(1)} %get-tuple-element.179, f32[512,2048]{1,0:T(8,128)S(1)} %get-tuple-element.180), kind=kLoop, calls=%fused_computation.11.clone.1 | loop fusion | flops 19922944 | bytes 16777216 | tf_op jit(solution)/shard_map/while/body/eval_jaxpr/jit(_where)/select_n | solution.py:16
  54.2 0.0 copy-done
  54.2 2.3 %fusion.12 = f32[3,512]{1,0:T(4,128)S(1)} fusion(f32[512,2048]{1,0:T(8,128)S(1)} %get-tuple-element.181, f32[3,2048]{1,0:T(4,128)S(1)} %get-tuple-element.178, f32[512,2048]{1,0:T(8,128)S(1)} %get-tuple-element.182, f32[3,2048]{1,0:T(4,128)S(1)} %get-tuple-element.177, f32[3,512]{1,0:T(4,128)S(1)} %copy-done), kind=kLoop, calls=%fused_computation.6.clone.1 | loop fusion | flops 15727104 | bytes 8450048 | tf_op jit(solution)/shard_map/while/body/eval_jaxpr/reduce_sum | solution.py:23
  56.5 8.2 %fusion.10 = (f32[512,2048]{1,0:T(8,128)S(1)}, f32[512,2048]{1,0:T(8,128)S(1)}) fusion(f32[3,2048]{1,0:T(4,128)S(1)} %get-tuple-element.177, f32[3,512]{1,0:T(4,128)} %get-tuple-element.203, f32[3,2048]{1,0:T(4,128)S(1)} %get-tuple-element.178), kind=kLoop, calls=%fused_computation.3.clone.1 | loop fusion | flops 13631488 | bytes 8443904 | tf_op jit(solution)/shard_map/while/body/eval_jaxpr/reduce_sum | solution.py:9
  64.7 0.0 copy-start
  64.7 3.6 %fusion.11 = (f32[512,2048]{1,0:T(8,128)S(1)}, f32[512,2048]{1,0:T(8,128)S(1)}) fusion(f32[512,2048]{1,0:T(8,128)S(1)} %get-tuple-element.179, f32[512,2048]{1,0:T(8,128)S(1)} %get-tuple-element.180), kind=kLoop, calls=%fused_computation.11.clone.1 | loop fusion | flops 19922944 | bytes 16777216 | tf_op jit(solution)/shard_map/while/body/eval_jaxpr/jit(_where)/select_n | solution.py:16
  68.3 0.0 copy-done
  68.3 2.3 %fusion.12 = f32[3,512]{1,0:T(4,128)S(1)} fusion(f32[512,2048]{1,0:T(8,128)S(1)} %get-tuple-element.181, f32[3,2048]{1,0:T(4,128)S(1)} %get-tuple-element.178, f32[512,2048]{1,0:T(8,128)S(1)} %get-tuple-element.182, f32[3,2048]{1,0:T(4,128)S(1)} %get-tuple-element.177, f32[3,512]{1,0:T(4,128)S(1)} %copy-done), kind=kLoop, calls=%fused_computation.6.clone.1 | loop fusion | flops 15727104 | bytes 8450048 | tf_op jit(solution)/shard_map/while/body/eval_jaxpr/reduce_sum | solution.py:23
  70.6 8.2 %fusion.10 = (f32[512,2048]{1,0:T(8,128)S(1)}, f32[512,2048]{1,0:T(8,128)S(1)}) fusion(f32[3,2048]{1,0:T(4,128)S(1)} %get-tuple-element.177, f32[3,512]{1,0:T(4,128)} %get-tuple-element.203, f32[3,2048]{1,0:T(4,128)S(1)} %get-tuple-element.178), kind=kLoop, calls=%fused_computation.3.clone.1 | loop fusion | flops 13631488 | bytes 8443904 | tf_op jit(solution)/shard_map/while/body/eval_jaxpr/reduce_sum | solution.py:9
  78.8 0.0 copy-start
  78.8 3.6 %fusion.11 = (f32[512,2048]{1,0:T(8,128)S(1)}, f32[512,2048]{1,0:T(8,128)S(1)}) fusion(f32[512,2048]{1,0:T(8,128)S(1)} %get-tuple-element.179, f32[512,2048]{1,0:T(8,128)S(1)} %get-tuple-element.180), kind=kLoop, calls=%fused_computation.11.clone.1 | loop fusion | flops 19922944 | bytes 16777216 | tf_op jit(solution)/shard_map/while/body/eval_jaxpr/jit(_where)/select_n | solution.py:16
  82.4 0.0 copy-done
  82.4 2.3 %fusion.12 = f32[3,512]{1,0:T(4,128)S(1)} fusion(f32[512,2048]{1,0:T(8,128)S(1)} %get-tuple-element.181, f32[3,2048]{1,0:T(4,128)S(1)} %get-tuple-element.178, f32[512,2048]{1,0:T(8,128)S(1)} %get-tuple-element.182, f32[3,2048]{1,0:T(4,128)S(1)} %get-tuple-element.177, f32[3,512]{1,0:T(4,128)S(1)} %copy-done), kind=kLoop, calls=%fused_computation.6.clone.1 | loop fusion | flops 15727104 | bytes 8450048 | tf_op jit(solution)/shard_map/while/body/eval_jaxpr/reduce_sum | solution.py:23
  84.7 8.2 %fusion.10 = (f32[512,2048]{1,0:T(8,128)S(1)}, f32[512,2048]{1,0:T(8,128)S(1)}) fusion(f32[3,2048]{1,0:T(4,128)S(1)} %get-tuple-element.177, f32[3,512]{1,0:T(4,128)} %get-tuple-element.203, f32[3,2048]{1,0:T(4,128)S(1)} %get-tuple-element.178), kind=kLoop, calls=%fused_computation.3.clone.1 | loop fusion | flops 13631488 | bytes 8443904 | tf_op jit(solution)/shard_map/while/body/eval_jaxpr/reduce_sum | solution.py:9
  92.9 0.0 copy-start
  92.9 3.6 %fusion.11 = (f32[512,2048]{1,0:T(8,128)S(1)}, f32[512,2048]{1,0:T(8,128)S(1)}) fusion(f32[512,2048]{1,0:T(8,128)S(1)} %get-tuple-element.179, f32[512,2048]{1,0:T(8,128)S(1)} %get-tuple-element.180), kind=kLoop, calls=%fused_computation.11.clone.1 | loop fusion | flops 19922944 | bytes 16777216 | tf_op jit(solution)/shard_map/while/body/eval_jaxpr/jit(_where)/select_n | solution.py:16
  96.5 0.0 copy-done
  96.5 2.3 %fusion.12 = f32[3,512]{1,0:T(4,128)S(1)} fusion(f32[512,2048]{1,0:T(8,128)S(1)} %get-tuple-element.181, f32[3,2048]{1,0:T(4,128)S(1)} %get-tuple-element.178, f32[512,2048]{1,0:T(8,128)S(1)} %get-tuple-element.182, f32[3,2048]{1,0:T(4,128)S(1)} %get-tuple-element.177, f32[3,512]{1,0:T(4,128)S(1)} %copy-done), kind=kLoop, calls=%fused_computation.6.clone.1 | loop fusion | flops 15727104 | bytes 8450048 | tf_op jit(solution)/shard_map/while/body/eval_jaxpr/reduce_sum | solution.py:23
  98.8 0.0 copy-done.1
  98.8 0.6 multiply_reduce_fusion.1
  99.4 31.7 %all-reduce = (f32[]{:T(128)}, f32[]{:T(128)}) all-reduce(f32[]{:T(128)} %get-tuple-element.119, f32[]{:T(128)} %get-tuple-element.118), channel_id=1, replica_groups=mesh['real'=2,'tile'=16] {'tile'}, use_global_device_ids=true, to_apply=%region_1.0 | all-reduce | flops 2 | bytes 16 | tf_op jit(solution)/shard_map/psum | solution.py:31
  132.5 0.6 multiply_reduce_fusion
  133.1 0.0 copy-start.2
  133.1 30.1 %psum.23 = f32[]{:T(128)} all-reduce(f32[]{:T(128)} %get-tuple-element.132), channel_id=1, replica_groups=mesh['real'=2,'tile'=16] {'tile'}, use_global_device_ids=true, to_apply=%region_10.11 | all-reduce | flops 1 | bytes 8 | tf_op jit(solution)/shard_map/psum | solution.py:50
  164.5 0.0 copy-done.3
  164.5 0.6 multiply_add_fusion
  165.1 0.0 copy-done.2
  (9 shorter events, 0.1 us)
Async XLA Ops:
  42.4 56.5 %copy-start.1 = (f32[3,512]{1,0:T(4,128)S(1)}, f32[3,512]{1,0:T(4,128)}, u32[]{:S(2)}) copy-start(f32[3,512]{1,0:T(4,128)} %param.6) | copy-start | bytes 18436
  42.4 122.2 %copy-start.3 = (f32[3,512]{1,0:T(4,128)S(1)}, f32[3,512]{1,0:T(4,128)}, u32[]{:S(2)}) copy-start(f32[3,512]{1,0:T(4,128)} %param.7) | copy-start | bytes 18436
  50.6 3.6 %copy-start = (f32[3,512]{1,0:T(4,128)S(1)}, f32[3,512]{1,0:T(4,128)}, u32[]{:S(2)}) copy-start(f32[3,512]{1,0:T(4,128)} %get-tuple-element.203) | copy-start | bytes 18436 | tf_op jit(solution)/shard_map/while
  64.7 3.6 %copy-start = (f32[3,512]{1,0:T(4,128)S(1)}, f32[3,512]{1,0:T(4,128)}, u32[]{:S(2)}) copy-start(f32[3,512]{1,0:T(4,128)} %get-tuple-element.203) | copy-start | bytes 18436 | tf_op jit(solution)/shard_map/while
  78.8 3.6 %copy-start = (f32[3,512]{1,0:T(4,128)S(1)}, f32[3,512]{1,0:T(4,128)}, u32[]{:S(2)}) copy-start(f32[3,512]{1,0:T(4,128)} %get-tuple-element.203) | copy-start | bytes 18436 | tf_op jit(solution)/shard_map/while
  92.9 3.6 %copy-start = (f32[3,512]{1,0:T(4,128)S(1)}, f32[3,512]{1,0:T(4,128)}, u32[]{:S(2)}) copy-start(f32[3,512]{1,0:T(4,128)} %get-tuple-element.203) | copy-start | bytes 18436 | tf_op jit(solution)/shard_map/while
  133.1 32.1 %copy-start.2 = (f32[3,512]{1,0:T(4,128)}, f32[3,512]{1,0:T(4,128)S(1)}, u32[]{:S(2)}) copy-start(f32[3,512]{1,0:T(4,128)S(1)} %get-tuple-element.133) | copy-start | bytes 18436
where the time goes:
time: 166 us; the launch traced here: 165 us
  blocking collectives  104 us (63%)
  other arithmetic  57.9 us (35%)
  between operations  3.34 us (2%)
    reduce_sum x4, other arithmetic, pair_terms(): squared = jnp.sum(separation * separation, axis=0)  32.7 us
    psum x1, blocking collectives, shards(): old_norm = lax.psum(jnp.sum(residual * residual), 'tile')  31.7 us
    psum x1, blocking collectives, shards(): new_norm = lax.psum(jnp.sum(new_residual * new_residual), 'tile')  30.1 us
    all_gather x1, blocking collectives, shards(): col_pos = lax.all_gather(positions, 'tile', axis=1, tiled=True)  23.7 us
    all_gather x1, blocking collectives, shards(): col_forces = lax.all_gather(residual, 'tile', axis=1, tiled=True)  18 us
    select_n x4, other arithmetic, pair_terms(): scalar_part = jnp.where(touching, 1.0 - 9.0 / 32.0 * radius, far_scalar)  14.3 us
    reduce_sum x4, other arithmetic, toward_rows(): jnp.sum(scalar_part[None] * col_forces[:, None, :] + (tensor_part * proje...  9.06 us

commit v1 on v0

v1 whole, which is shorter than its diff:
```python
import functools
import math

import jax
import jax.numpy as jnp
from jax import lax
from jax.experimental import pallas as pl
from jax.experimental.pallas import tpu as pltpu
from jax.sharding import PartitionSpec as P

MESH = pl.DeviceIdType.MESH
CENTRE = 62.0
SCALE = math.sqrt(0.75)
TOUCH = math.sqrt(3.0)
FACTOR = SCALE**3 / 2.0
ROWS = 128
KDIM = 64


def split3(x):
    high = x.astype(jnp.bfloat16).astype(jnp.float32)
    rest = x - high
    mid = rest.astype(jnp.bfloat16).astype(jnp.float32)
    return high, mid, rest - mid


def split2(x):
    high = x.astype(jnp.bfloat16)
    return high, (x - high.astype(jnp.float32)).astype(jnp.bfloat16)


def dot_nn(a, b):
    return lax.dot_general(a, b, (((1,), (0,)), ((), ())), preferred_element_type=jnp.float32)


def dot_nt(a, b):
    return lax.dot_general(a, b, (((1,), (1,)), ((), ())), preferred_element_type=jnp.float32)


def features(x):
    high, mid, low = split3(x)
    row = lax.broadcasted_iota(jnp.int32, x.shape, 0)
    ones = jnp.where(row < 3, 1.0, 0.0).astype(jnp.float32)
    return jnp.concatenate(
        [high, mid, low, high, mid, high, ones, jnp.zeros_like(x)], axis=0
    ).astype(jnp.bfloat16)


def own_features(x):
    high, mid, low = split3(x)
    row = lax.broadcasted_iota(jnp.int32, x.shape, 0)
    zero = jnp.zeros_like(x)
    is_pos = row < 3
    near = [jnp.where(is_pos, -2.0 * part, zero) for part in (high, mid, low)]
    near[0] = jnp.where(row == 3, 1.0, near[0])
    shifted = [jnp.where((row >= 4) & (row < 7), pltpu.roll(part, 4, 0), zero) for part in (high, mid, low)]
    shifted[0] = jnp.where(row == 7, -1.0, shifted[0])
    own = jnp.where(row == 0, high[3:4], jnp.where(row == 1, mid[3:4], jnp.where(row == 2, low[3:4], zero)))

    def stack(parts, last):
        h, m, l = parts
        return jnp.concatenate([h, h, h, m, m, l, last, zero], axis=0)

    both = jnp.concatenate([stack(near, own), stack(shifted, zero)], axis=0)
    return both.T


def pair_block(cols, own_ref, acc_f, acc_g, diagonal):
    size = own_ref.shape[1]
    for start in range(0, size, ROWS):
        rows = slice(start, start + ROWS)
        squared = dot_nn(own_ref[0, rows, :], cols)
        projected = dot_nn(own_ref[1, rows, :], cols)
        if diagonal:
            i = lax.broadcasted_iota(jnp.int32, squared.shape, 0) + start
            j = lax.broadcasted_iota(jnp.int32, squared.shape, 1)
            squared = jnp.where(i == j, 0.0, squared)
            projected = jnp.where(i == j, 0.0, projected)
            inverse = lax.rsqrt(jnp.maximum(squared, 0.25 * SCALE * SCALE))
        else:
            inverse = lax.rsqrt(squared)
        capped = jnp.minimum(inverse, 1.0 / TOUCH)
        capped_sq = capped * capped
        scalar = capped * (2.0 + capped_sq) + jnp.maximum(TOUCH - squared * inverse, 0.0)
        tensor = (capped_sq * (2.0 / 3.0 - capped_sq)) * (inverse * projected)
        s_high, s_low = split2(scalar)
        t_high, t_low = split2(tensor)
        acc_f[rows, :] += dot_nt(s_high, cols) + dot_nt(s_low, cols)
        acc_g[rows, :] += dot_nt(t_high, cols) + dot_nt(t_low, cols)


def delta_of(k, n):
    return (k % 2) * ((k + 1) // 2) + (1 - k % 2) * (n - k // 2)


def kernel(
    n, p_ref, f_ref, it_ref, o_it, o_res, o_dir,
    gath, own_ref, acc_f, acc_g, stat, send_sem, recv_sem, stat_send, stat_recv,
):
    me = lax.axis_index("tile")
    barrier = pltpu.get_barrier_semaphore()

    def peer(k):
        return {"tile": lax.rem(me + delta_of(k, n), n)}

    def source(k):
        return lax.rem(me + n - delta_of(k, n), n)

    @pl.loop(1, n)
    def _(k):
        pl.semaphore_signal(barrier, inc=1, device_id=peer(k), device_id_type=MESH)

    pos = (p_ref[...] - CENTRE) * SCALE
    force = f_ref[...]
    gath[me, 0:3, :] = pos
    gath[me, 3:4, :] = jnp.sum(pos * pos, axis=0, keepdims=True)
    gath[me, 4:7, :] = force
    gath[me, 7:8, :] = jnp.sum(pos * force, axis=0, keepdims=True)

    x = gath[me]
    own_cols = features(x)
    own_t = own_features(x)
    own_ref[0, :, :] = own_t[:, :KDIM].astype(jnp.bfloat16)
    own_ref[1, :, :] = own_t[:, KDIM:].astype(jnp.bfloat16)
    acc_f[...] = jnp.zeros_like(acc_f)
    acc_g[...] = jnp.zeros_like(acc_g)

    pl.semaphore_wait(barrier, n - 1)

    def block_copy(k):
        return pltpu.make_async_remote_copy(
            src_ref=gath.at[me], dst_ref=gath.at[me], send_sem=send_sem.at[k], recv_sem=recv_sem.at[k],
            device_id=peer(k), device_id_type=MESH,
        )

    def block_arrival(k):
        return pltpu.make_async_remote_copy(
            src_ref=gath.at[source(k)], dst_ref=gath.at[source(k)], send_sem=send_sem.at[k], recv_sem=recv_sem.at[k],
            device_id=peer(k), device_id_type=MESH,
        )

    @pl.loop(1, n)
    def _(k):
        block_copy(k).start()

    pair_block(own_cols, own_ref, acc_f, acc_g, True)

    @pl.loop(1, n)
    def _(k):
        block_arrival(k).wait_recv()
        pair_block(features(gath[source(k)]), own_ref, acc_f, acc_g, False)

    sum_f = acc_f[...].T
    sum_g = acc_g[...].T
    c_part = sum_f[4:7] + (sum_f[12:15] + sum_f[20:23])
    g_pos = sum_g[0:3] + (sum_g[8:11] + sum_g[16:19])
    g_all = sum_g[48:49]
    image = FACTOR * (c_part + 3.0 * (pos * g_all - g_pos))

    def lanes(v):
        total = jnp.sum(v, axis=0, keepdims=True)
        part = total[:, 0:128]
        for s in range(128, total.shape[1], 128):
            part = part + total[:, s : s + 128]
        return part

    row = lax.broadcasted_iota(jnp.int32, (8, 128), 0)
    stat[me] = jnp.where(
        row == 0, lanes(force * force),
        jnp.where(row == 1, lanes(force * image), jnp.where(row == 2, lanes(image * image), 0.0)),
    )

    def stat_copy(k):
        return pltpu.make_async_remote_copy(
            src_ref=stat.at[me], dst_ref=stat.at[me], send_sem=stat_send.at[k], recv_sem=stat_recv.at[k],
            device_id=peer(k), device_id_type=MESH,
        )

    def stat_arrival(k):
        return pltpu.make_async_remote_copy(
            src_ref=stat.at[source(k)], dst_ref=stat.at[source(k)], send_sem=stat_send.at[k], recv_sem=stat_recv.at[k],
            device_id=peer(k), device_id_type=MESH,
        )

    @pl.loop(1, n)
    def _(k):
        stat_copy(k).start()

    @pl.loop(1, n)
    def _(k):
        block_copy(k).wait_send()

    @pl.loop(1, n)
    def _(k):
        stat_arrival(k).wait_recv()

    total = jnp.sum(stat[...], axis=0)
    total = jnp.sum(total, axis=1, keepdims=True)
    old_norm = total[0:1]
    step = old_norm / total[1:2]
    new_norm = step * step * total[2:3] - old_norm
    new_residual = force - step * image
    o_it[...] = it_ref[...] + step * force
    o_res[...] = new_residual
    o_dir[...] = new_residual + (new_norm / old_norm) * force

    @pl.loop(1, n)
    def _(k):
        stat_copy(k).wait_send()


def solution(mesh):
    n = mesh.shape["tile"]

    def shards(positions, residual, iterate):
        dims, size = positions.shape
        out = jax.ShapeDtypeStruct((dims, size), jnp.float32)
        spec = pl.BlockSpec(memory_space=pltpu.VMEM)
        return pl.pallas_call(
            functools.partial(kernel, n),
            out_shape=(out, out, out),
            in_specs=[spec] * 3,
            out_specs=(spec,) * 3,
            scratch_shapes=[
                pltpu.VMEM((n, 8, size), jnp.float32),
                pltpu.VMEM((2, size, KDIM), jnp.bfloat16),
                pltpu.VMEM((size, KDIM), jnp.float32),
                pltpu.VMEM((size, KDIM), jnp.float32),
                pltpu.VMEM((n, 8, 128), jnp.float32),
                pltpu.SemaphoreType.DMA((n,)),
                pltpu.SemaphoreType.DMA((n,)),
                pltpu.SemaphoreType.DMA((n,)),
                pltpu.SemaphoreType.DMA((n,)),
            ],
            compiler_params=pltpu.CompilerParams(collective_id=0, has_side_effects=True),
        )(positions, residual, iterate)

    spec = P("real", "tile")
    return jax.shard_map(
        shards, mesh=mesh, in_specs=(spec, spec, spec), out_specs=(spec, spec, spec), check_vma=False
    )
```

time: 166 us -> 42.3 us (0.25)
  blocking collectives: 104 us -> 0 us
  other arithmetic: 57.9 us -> 0 us
  Pallas kernels: 0 us -> 38.6 us
  between operations: 3.34 us -> 0.65 us
  local copies, waits for them, and re-layouts: 0.11 us -> 2.61 us
    psum x2 -> x0, blocking collectives: 61.8 us -> none  [the longest x1 31.7 us: shards(): old_norm = lax.psum(jnp.sum(residual * residual), 'tile')]
    reduce_sum x10 -> x0, other arithmetic: 42.9 us -> none  [the longest x4 32.7 us: pair_terms(): squared = jnp.sum(separation * separation, axis=0)]
    all_gather x2 -> x0, blocking collectives: 41.7 us -> none  [the longest x1 23.7 us: shards(): col_pos = lax.all_gather(positions, 'tile', axis=1, tiled=True)]
    pallas_call x0 -> x1, Pallas kernels: none -> 38.6 us  [shards(): pl.pallas_call(functools.partial(kernel, n), out_shape=(out, out, out), i...]
    select_n x4 -> x0, other arithmetic: 14.3 us -> none  [pair_terms(): scalar_part = jnp.where(touching, 1.0 - 9.0 / 32.0 * radius, far_scalar)]
    unnamed x6 -> x7, local copies, waits for them, and re-layouts: 0.01 us -> 2.61 us
where the time goes in v1:
time: 42.3 us; the launch traced here: 41.9 us
  Pallas kernels  38.6 us (91%)
  local copies, waits for them, and re-layouts  2.61 us (6%)
  between operations  0.65 us (2%)
    pallas_call x1, Pallas kernels, shards(): pl.pallas_call(functools.partial(kernel, n), out_shape=(out, out, out), i...  38.6 us
    unnamed x7, local copies, waits for them, and re-layouts  2.61 us

profile of v1, /device:TPU:0, one launch (start us, length us, event | category | flops | bytes accessed | tf_op | source)
XLA Modules:
  0.0 41.9 jit_solution(6611027688867170552)
XLA Ops:
  0.6 38.6 %shard_map.58 = (f32[3,512]{1,0:T(4,128)}, f32[3,512]{1,0:T(4,128)}, f32[3,512]{1,0:T(4,128)}) custom-call(f32[3,512]{1,0:T(4,128)} %p_ref.1, f32[3,512]{1,0:T(4,128)} %f_ref.1, f32[3,512]{1,0:T(4,128)} %it_ref.1), custom_call_target="tpu_custom_call" | custom-call | tf_op jit(solution)/shard_map/pallas_call | solution.py:219
  39.3 0.0 copy-start.1
  39.3 1.3 %copy.9 = f32[3,512]{1,0:T(4,128)} copy(f32[3,512]{1,0:T(4,128)} %get-tuple-element.6) | data formatting | bytes 12288
  40.6 0.0 copy-done.1
  40.6 0.0 copy-start
  40.6 0.6 %copy.10 = f32[3,512]{1,0:T(4,128)} copy(f32[3,512]{1,0:T(4,128)S(1)} %copy-done.1) | data formatting | bytes 12288
  41.2 0.1 copy-done
  41.3 0.6 %copy.11 = f32[3,512]{1,0:T(4,128)} copy(f32[3,512]{1,0:T(4,128)S(1)} %copy-done) | data formatting | bytes 12288
Async XLA Ops:
  39.3 1.3 %copy-start.1 = (f32[3,512]{1,0:T(4,128)S(1)}, f32[3,512]{1,0:T(4,128)}, u32[]{:S(2)}) copy-start(f32[3,512]{1,0:T(4,128)} %get-tuple-element.7) | copy-start | bytes 18436
  40.6 0.7 %copy-start = (f32[3,512]{1,0:T(4,128)S(1)}, f32[3,512]{1,0:T(4,128)}, u32[]{:S(2)}) copy-start(f32[3,512]{1,0:T(4,128)} %get-tuple-element.8) | copy-start | bytes 18436

commit v2 on v1

v2 whole, which is shorter than its diff:
```python
import functools
import math

import jax
import jax.numpy as jnp
from jax import lax
from jax.experimental import pallas as pl
from jax.experimental.pallas import tpu as pltpu
from jax.sharding import PartitionSpec as P

MESH = pl.DeviceIdType.MESH
CENTRE = 62.0
SCALE = math.sqrt(0.75)
TOUCH = math.sqrt(3.0)
FACTOR = SCALE**3 / 2.0
ROWS = 128
KDIM = 64


def split3(x):
    high = x.astype(jnp.bfloat16).astype(jnp.float32)
    rest = x - high
    mid = rest.astype(jnp.bfloat16).astype(jnp.float32)
    return high, mid, rest - mid


def split2(x):
    high = x.astype(jnp.bfloat16)
    return high, (x - high.astype(jnp.float32)).astype(jnp.bfloat16)


def dot_nn(a, b):
    return lax.dot_general(a, b, (((1,), (0,)), ((), ())), preferred_element_type=jnp.float32)


def dot_nt(a, b):
    return lax.dot_general(a, b, (((1,), (1,)), ((), ())), preferred_element_type=jnp.float32)


def columns(x):
    high, mid, low = split3(x)
    row = lax.broadcasted_iota(jnp.int32, x.shape, 0)
    ones = jnp.where(row < 3, 1.0, 0.0).astype(jnp.float32)
    return jnp.concatenate(
        [high, mid, low, high, mid, high, ones, jnp.zeros_like(x)], axis=0
    ).astype(jnp.bfloat16)


def weights(x):
    row = lax.broadcasted_iota(jnp.int32, x.shape, 0)
    doubled = jnp.where(row < 4, pltpu.roll(x, 4, 0), x)
    first = doubled * jnp.where(row < 4, x[0:1], 1.0)
    second = doubled * jnp.where(row < 4, x[1:2], x[2:3])
    zero = jnp.zeros_like(x)
    return jnp.concatenate([*split3(first), *split3(second), zero, zero], axis=0).astype(jnp.bfloat16)


def own_rows(x):
    high, mid, low = split3(x)
    row = lax.broadcasted_iota(jnp.int32, x.shape, 0)
    zero = jnp.zeros_like(x)
    h, m, l = [jnp.where(row < 3, -2.0 * part, zero) for part in (high, mid, low)]
    h = jnp.where(row == 3, 1.0, h)
    own = jnp.where(row == 0, high[3:4], jnp.where(row == 1, mid[3:4], jnp.where(row == 2, low[3:4], zero)))
    return jnp.concatenate([h, h, h, m, m, l, own, zero] + [zero] * 8, axis=0).T


def combine(sum_f, sum_h, pos):
    scalar = sum_f[4:7] + (sum_f[12:15] + sum_f[20:23])
    first = sum_h[0:8] + (sum_h[8:16] + sum_h[16:24])
    second = sum_h[24:32] + (sum_h[32:40] + sum_h[40:48])
    along = jnp.sum(pos * first[4:7], axis=0, keepdims=True) - first[7:8]
    mixed = jnp.concatenate(
        [
            part[3:4] - jnp.sum(pos * part[0:3], axis=0, keepdims=True)
            for part in (first[0:4], second[0:4], second[4:8])
        ],
        axis=0,
    )
    return scalar + 3.0 * (pos * along + mixed)


def pair_block(x, own_ref, own_weights, acc_f, acc_h, far_f, far_h, diagonal):
    size = own_ref.shape[0]
    cols = columns(x)
    wide = weights(x)
    twice = jnp.concatenate([wide, wide], axis=1)
    for start in range(0, size, ROWS):
        rows = slice(start, start + ROWS)
        squared = dot_nn(own_ref[rows, :], cols)
        if diagonal:
            i = lax.broadcasted_iota(jnp.int32, squared.shape, 0) + start
            j = lax.broadcasted_iota(jnp.int32, squared.shape, 1)
            squared = jnp.where(i == j, 0.0, squared)
            inverse = lax.rsqrt(jnp.maximum(squared, 0.25 * SCALE * SCALE))
        else:
            inverse = lax.rsqrt(squared)
        capped = jnp.minimum(inverse, 1.0 / TOUCH)
        capped_sq = capped * capped
        scalar = capped * (2.0 + capped_sq) + jnp.maximum(TOUCH - squared * inverse, 0.0)
        tensor = (capped_sq * (2.0 / 3.0 - capped_sq)) * inverse
        if diagonal:
            tensor = jnp.where(i == j, 0.0, tensor)
        s_high, s_low = split2(scalar)
        t_high, t_low = split2(tensor)
        acc_f[rows, :] += dot_nt(jnp.concatenate([s_high, s_low], axis=1), twice)
        acc_h[rows, :] += dot_nt(jnp.concatenate([t_high, t_low], axis=1), twice)
        if far_f is not None:
            own = own_weights[:, rows]
            own = jnp.concatenate([own, own], axis=1)
            out_f = dot_nn(own, jnp.concatenate([s_high, s_low], axis=0))
            out_h = dot_nn(own, jnp.concatenate([t_high, t_low], axis=0))
            if start == 0:
                far_f[...] = out_f
                far_h[...] = out_h
            else:
                far_f[...] += out_f
                far_h[...] += out_h


def kernel(
    n, p_ref, f_ref, it_ref, o_it, o_res, o_dir,
    gath, own_ref, own_w, acc_f, acc_h, far_f, far_h, give, take, stat,
    send_sem, recv_sem, give_sem, take_sem, stat_send, stat_recv,
):
    me = lax.axis_index("tile")
    half = n // 2
    barrier = pltpu.get_barrier_semaphore()

    def ahead(k):
        return lax.rem(me + k, n)

    def behind(k):
        return lax.rem(me + n - k, n)

    @pl.loop(1, n)
    def _(k):
        pl.semaphore_signal(barrier, inc=1, device_id={"tile": ahead(k)}, device_id_type=MESH)

    pos = (p_ref[...] - CENTRE) * SCALE
    force = f_ref[...]
    gath[me, 0:3, :] = pos
    gath[me, 3:4, :] = jnp.sum(pos * pos, axis=0, keepdims=True)
    gath[me, 4:7, :] = force
    gath[me, 7:8, :] = jnp.sum(pos * force, axis=0, keepdims=True)

    x = gath[me]
    own_ref[...] = own_rows(x)[:, :KDIM].astype(jnp.bfloat16)
    own_w[...] = weights(x)
    acc_f[...] = jnp.zeros_like(acc_f)
    acc_h[...] = jnp.zeros_like(acc_h)

    pl.semaphore_wait(barrier, n - 1)

    def block_copy(k, slot):
        return pltpu.make_async_remote_copy(
            src_ref=gath.at[slot], dst_ref=gath.at[slot], send_sem=send_sem.at[k], recv_sem=recv_sem.at[k],
            device_id={"tile": behind(k)}, device_id_type=MESH,
        )

    def give_copy(k):
        return pltpu.make_async_remote_copy(
            src_ref=give.at[k], dst_ref=take.at[k], send_sem=give_sem.at[k], recv_sem=take_sem.at[k],
            device_id={"tile": ahead(k)}, device_id_type=MESH,
        )

    def stat_copy(k, slot):
        return pltpu.make_async_remote_copy(
            src_ref=stat.at[slot], dst_ref=stat.at[slot], send_sem=stat_send.at[k], recv_sem=stat_recv.at[k],
            device_id={"tile": ahead(k)}, device_id_type=MESH,
        )

    @pl.loop(1, half + 1)
    def _(k):
        block_copy(k, me).start()

    pair_block(x, own_ref, own_w, acc_f, acc_h, None, None, True)

    @pl.loop(1, half)
    def _(k):
        block_copy(k, ahead(k)).wait_recv()

        @pl.when(k > 1)
        def _():
            give_copy(k - 1).start()

        other = gath[ahead(k)]
        pair_block(other, own_ref, own_w, acc_f, acc_h, far_f, far_h, False)
        give[k, 0:3, :] = combine(far_f[...], far_h[...], other[0:3])

    block_copy(half, ahead(half)).wait_recv()
    if half > 1:
        give_copy(half - 1).start()
    pair_block(gath[ahead(half)], own_ref, own_w, acc_f, acc_h, None, None, False)

    image = combine(acc_f[...].T, acc_h[...].T, pos)

    def added(k, running):
        give_copy(k).wait_recv()
        return running + take[k, 0:3, :]

    image = FACTOR * lax.fori_loop(1, half, added, image)

    def lanes(v):
        total = jnp.sum(v, axis=0, keepdims=True)
        part = total[:, 0:128]
        for s in range(128, total.shape[1], 128):
            part = part + total[:, s : s + 128]
        return part

    row = lax.broadcasted_iota(jnp.int32, (8, 128), 0)
    stat[me] = jnp.where(
        row == 0, lanes(force * force),
        jnp.where(row == 1, lanes(force * image), jnp.where(row == 2, lanes(image * image), 0.0)),
    )

    @pl.loop(1, n)
    def _(k):
        stat_copy(k, me).start()

    @pl.loop(1, half + 1)
    def _(k):
        block_copy(k, me).wait_send()

    @pl.loop(1, half)
    def _(k):
        give_copy(k).wait_send()

    @pl.loop(1, n)
    def _(k):
        stat_copy(k, behind(k)).wait_recv()

    total = jnp.sum(stat[...], axis=0)
    total = jnp.sum(total, axis=1, keepdims=True)
    old_norm = total[0:1]
    step = old_norm / total[1:2]
    new_norm = step * step * total[2:3] - old_norm
    new_residual = force - step * image
    o_it[...] = it_ref[...] + step * force
    o_res[...] = new_residual
    o_dir[...] = new_residual + (new_norm / old_norm) * force

    @pl.loop(1, n)
    def _(k):
        stat_copy(k, me).wait_send()


def solution(mesh):
    n = mesh.shape["tile"]

    def shards(positions, residual, iterate):
        dims, size = positions.shape
        out = jax.ShapeDtypeStruct((dims, size), jnp.float32)
        spec = pl.BlockSpec(memory_space=pltpu.VMEM)
        return pl.pallas_call(
            functools.partial(kernel, n),
            out_shape=(out, out, out),
            in_specs=[spec] * 3,
            out_specs=(spec,) * 3,
            scratch_shapes=[
                pltpu.VMEM((n, 8, size), jnp.float32),
                pltpu.VMEM((size, KDIM), jnp.bfloat16),
                pltpu.VMEM((KDIM, size), jnp.bfloat16),
                pltpu.VMEM((size, KDIM), jnp.float32),
                pltpu.VMEM((size, KDIM), jnp.float32),
                pltpu.VMEM((KDIM, size), jnp.float32),
                pltpu.VMEM((KDIM, size), jnp.float32),
                pltpu.VMEM((n // 2, 8, size), jnp.float32),
                pltpu.VMEM((n // 2, 8, size), jnp.float32),
                pltpu.VMEM((n, 8, 128), jnp.float32),
                pltpu.SemaphoreType.DMA((n // 2 + 1,)),
                pltpu.SemaphoreType.DMA((n // 2 + 1,)),
                pltpu.SemaphoreType.DMA((n // 2,)),
                pltpu.SemaphoreType.DMA((n // 2,)),
                pltpu.SemaphoreType.DMA((n,)),
                pltpu.SemaphoreType.DMA((n,)),
            ],
            compiler_params=pltpu.CompilerParams(collective_id=0, has_side_effects=True),
        )(positions, residual, iterate)

    spec = P("real", "tile")
    return jax.shard_map(
        shards, mesh=mesh, in_specs=(spec, spec, spec), out_specs=(spec, spec, spec), check_vma=False
    )
```

time: 42.3 us -> 34.8 us (0.82)
  Pallas kernels: 38.6 us -> 31.2 us
    pallas_call x1, Pallas kernels: 38.6 us -> 31.2 us  [shards(): pl.pallas_call(functools.partial(kernel, n), out_shape=(out, out, out), i...]
where the time goes in v2:
time: 34.8 us; the launch traced here: 34.4 us
  Pallas kernels  31.2 us (90%)
  local copies, waits for them, and re-layouts  2.61 us (8%)
  between operations  0.65 us (2%)
    pallas_call x1, Pallas kernels, shards(): pl.pallas_call(functools.partial(kernel, n), out_shape=(out, out, out), i...  31.2 us
    unnamed x7, local copies, waits for them, and re-layouts  2.61 us

profile of v2, /device:TPU:0, one launch (start us, length us, event | category | flops | bytes accessed | tf_op | source)
XLA Modules:
  0.0 34.4 jit_solution(8669492166864894481)
XLA Ops:
  0.6 31.2 %shard_map.58 = (f32[3,512]{1,0:T(4,128)}, f32[3,512]{1,0:T(4,128)}, f32[3,512]{1,0:T(4,128)}) custom-call(f32[3,512]{1,0:T(4,128)} %p_ref.1, f32[3,512]{1,0:T(4,128)} %f_ref.1, f32[3,512]{1,0:T(4,128)} %it_ref.1), custom_call_target="tpu_custom_call" | custom-call | tf_op jit(solution)/shard_map/pallas_call | solution.py:255
  31.8 0.0 copy-start.1
  31.8 1.3 %copy.9 = f32[3,512]{1,0:T(4,128)} copy(f32[3,512]{1,0:T(4,128)} %get-tuple-element.6) | data formatting | bytes 12288
  33.1 0.0 copy-done.1
  33.1 0.0 copy-start
  33.1 0.6 %copy.10 = f32[3,512]{1,0:T(4,128)} copy(f32[3,512]{1,0:T(4,128)S(1)} %copy-done.1) | data formatting | bytes 12288
  33.7 0.1 copy-done
  33.8 0.6 %copy.11 = f32[3,512]{1,0:T(4,128)} copy(f32[3,512]{1,0:T(4,128)S(1)} %copy-done) | data formatting | bytes 12288
Async XLA Ops:
  31.8 1.3 %copy-start.1 = (f32[3,512]{1,0:T(4,128)S(1)}, f32[3,512]{1,0:T(4,128)}, u32[]{:S(2)}) copy-start(f32[3,512]{1,0:T(4,128)} %get-tuple-element.7) | copy-start | bytes 18436
  33.1 0.7 %copy-start = (f32[3,512]{1,0:T(4,128)S(1)}, f32[3,512]{1,0:T(4,128)}, u32[]{:S(2)}) copy-start(f32[3,512]{1,0:T(4,128)} %get-tuple-element.8) | copy-start | bytes 18436

commit v3 on v2

--- a/solution.py
+++ b/solution.py
@@ -13,7 +13,8 @@
 SCALE = math.sqrt(0.75)
 TOUCH = math.sqrt(3.0)
 FACTOR = SCALE**3 / 2.0
-ROWS = 128
+ROWS = 512
+AHEAD = 2
 KDIM = 64
 
 
@@ -119,7 +120,7 @@
 
 
 def kernel(
-    n, p_ref, f_ref, it_ref, o_it, o_res, o_dir,
+    n, p_ref, f_ref, o_image, o_step, o_ratio,
     gath, own_ref, own_w, acc_f, acc_h, far_f, far_h, give, take, stat,
     send_sem, recv_sem, give_sem, take_sem, stat_send, stat_recv,
 ):
@@ -170,7 +171,7 @@
             device_id={"tile": ahead(k)}, device_id_type=MESH,
         )
 
-    @pl.loop(1, half + 1)
+    @pl.loop(1, min(AHEAD, half) + 1)
     def _(k):
         block_copy(k, me).start()
 
@@ -178,6 +179,10 @@
 
     @pl.loop(1, half)
     def _(k):
+        @pl.when(k + AHEAD <= half)
+        def _():
+            block_copy(k + AHEAD, me).start()
+
         block_copy(k, ahead(k)).wait_recv()
 
         @pl.when(k > 1)
@@ -186,7 +191,7 @@
 
         other = gath[ahead(k)]
         pair_block(other, own_ref, own_w, acc_f, acc_h, far_f, far_h, False)
-        give[k, 0:3, :] = combine(far_f[...], far_h[...], other[0:3])
+        give[k] = combine(far_f[...], far_h[...], other[0:3])
 
     block_copy(half, ahead(half)).wait_recv()
     if half > 1:
@@ -197,21 +202,17 @@
 
     def added(k, running):
         give_copy(k).wait_recv()
-        return running + take[k, 0:3, :]
+        return running + take[k]
 
     image = FACTOR * lax.fori_loop(1, half, added, image)
 
-    def lanes(v):
-        total = jnp.sum(v, axis=0, keepdims=True)
-        part = total[:, 0:128]
-        for s in range(128, total.shape[1], 128):
-            part = part + total[:, s : s + 128]
-        return part
-
-    row = lax.broadcasted_iota(jnp.int32, (8, 128), 0)
+    def whole(v):
+        return jnp.sum(jnp.sum(v, axis=0, keepdims=True), axis=1, keepdims=True)
+
+    lane = lax.broadcasted_iota(jnp.int32, (1, 128), 1)
     stat[me] = jnp.where(
-        row == 0, lanes(force * force),
-        jnp.where(row == 1, lanes(force * image), jnp.where(row == 2, lanes(image * image), 0.0)),
+        lane == 0, whole(force * force),
+        jnp.where(lane == 1, whole(force * image), jnp.where(lane == 2, whole(image * image), 0.0)),
     )
 
     @pl.loop(1, n)
@@ -231,14 +232,12 @@
         stat_copy(k, behind(k)).wait_recv()
 
     total = jnp.sum(stat[...], axis=0)
-    total = jnp.sum(total, axis=1, keepdims=True)
-    old_norm = total[0:1]
-    step = old_norm / total[1:2]
-    new_norm = step * step * total[2:3] - old_norm
-    new_residual = force - step * image
-    o_it[...] = it_ref[...] + step * force
-    o_res[...] = new_residual
-    o_dir[...] = new_residual + (new_norm / old_norm) * force
+    old_norm = total[:, 0:1]
+    step = old_norm / total[:, 1:2]
+    new_norm = step * step * total[:, 2:3] - old_norm
+    o_image[...] = image
+    o_step[...] = jnp.broadcast_to(step, image.shape)
+    o_ratio[...] = jnp.broadcast_to(new_norm / old_norm, image.shape)
 
     @pl.loop(1, n)
     def _(k):
@@ -252,10 +251,10 @@
         dims, size = positions.shape
         out = jax.ShapeDtypeStruct((dims, size), jnp.float32)
         spec = pl.BlockSpec(memory_space=pltpu.VMEM)
-        return pl.pallas_call(
+        image, step, ratio = pl.pallas_call(
             functools.partial(kernel, n),
             out_shape=(out, out, out),
-            in_specs=[spec] * 3,
+            in_specs=[spec] * 2,
             out_specs=(spec,) * 3,
             scratch_shapes=[
                 pltpu.VMEM((n, 8, size), jnp.float32),
@@ -265,9 +264,9 @@
                 pltpu.VMEM((size, KDIM), jnp.float32),
                 pltpu.VMEM((KDIM, size), jnp.float32),
                 pltpu.VMEM((KDIM, size), jnp.float32),
-                pltpu.VMEM((n // 2, 8, size), jnp.float32),
-                pltpu.VMEM((n // 2, 8, size), jnp.float32),
-                pltpu.VMEM((n, 8, 128), jnp.float32),
+                pltpu.VMEM((n // 2, 3, size), jnp.float32),
+                pltpu.VMEM((n // 2, 3, size), jnp.float32),
+                pltpu.VMEM((n, 1, 128), jnp.float32),
                 pltpu.SemaphoreType.DMA((n // 2 + 1,)),
                 pltpu.SemaphoreType.DMA((n // 2 + 1,)),
                 pltpu.SemaphoreType.DMA((n // 2,)),
@@ -276,7 +275,9 @@
                 pltpu.SemaphoreType.DMA((n,)),
             ],
             compiler_params=pltpu.CompilerParams(collective_id=0, has_side_effects=True),
-        )(positions, residual, iterate)
+        )(positions, residual)
+        new_residual = residual - step * image
+        return iterate + step * residual, new_residual, new_residual + ratio * residual
 
     spec = P("real", "tile")
     return jax.shard_map(

time: 34.8 us -> 30.7 us (0.88)
  Pallas kernels: 31.2 us -> 28.4 us
  local copies, waits for them, and re-layouts: 2.61 us -> 0.01 us
  other arithmetic: 0 us -> 1.34 us
    pallas_call x1, Pallas kernels: 31.2 us -> 28.4 us  [shards(): pl.pallas_call(functools.partial(kernel, n), out_shape=(out, out, out), i...]
    unnamed x7 -> x4, local copies, waits for them, and re-layouts: 2.61 us -> 0.01 us
    add x0 -> x1, other arithmetic: none -> 1.34 us  [shards(): new_residual + ratio * residual]
where the time goes in v3:
time: 30.7 us; the launch traced here: 30.4 us
  Pallas kernels  28.4 us (93%)
  other arithmetic  1.34 us (4%)
  between operations  0.67 us (2%)
    pallas_call x1, Pallas kernels, shards(): pl.pallas_call(functools.partial(kernel, n), out_shape=(out, out, out), i...  28.4 us
    add x1, other arithmetic, shards(): new_residual + ratio * residual  1.34 us

profile of v3, /device:TPU:0, one launch (start us, length us, event | category | flops | bytes accessed | tf_op | source)
XLA Modules:
  0.0 30.4 jit_solution(1431676826695082194)
XLA Ops:
  0.6 0.0 copy-start
  0.6 0.0 copy-start.1
  0.7 28.4 %shard_map.58 = (f32[3,512]{1,0:T(4,128)}, f32[3,512]{1,0:T(4,128)}, f32[3,512]{1,0:T(4,128)}) custom-call(f32[3,512]{1,0:T(4,128)} %p_ref.1, f32[3,512]{1,0:T(4,128)} %f_ref.1), custom_call_target="tpu_custom_call" | custom-call | tf_op jit(solution)/shard_map/pallas_call | solution.py:254
  29.1 0.0 copy-done
  29.1 0.0 copy-done.1
  29.1 1.3 %multiply_add_fusion = (f32[3,512]{1,0:T(4,128)}, f32[3,512]{1,0:T(4,128)}, f32[3,512]{1,0:T(4,128)}) fusion(f32[3,512]{1,0:T(4,128)} %get-tuple-element.8, f32[3,512]{1,0:T(4,128)S(1)} %copy-done, f32[3,512]{1,0:T(4,128)} %get-tuple-element.6, f32[3,512]{1,0:T(4,128)} %get-tuple-element.7, f32[3,512]{1,0:T(4,128)S(1)} %copy-done.1), kind=kLoop, calls=%fused_computation | loop fusion | flops 9216 | bytes 49152 | tf_op jit(solution)/shard_map/add | solution.py:280
Async XLA Ops:
  0.6 28.4 %copy-start = (f32[3,512]{1,0:T(4,128)S(1)}, f32[3,512]{1,0:T(4,128)}, u32[]{:S(2)}) copy-start(f32[3,512]{1,0:T(4,128)} %f_ref.1) | copy-start | bytes 18436
  0.6 28.4 %copy-start.1 = (f32[3,512]{1,0:T(4,128)S(1)}, f32[3,512]{1,0:T(4,128)}, u32[]{:S(2)}) copy-start(f32[3,512]{1,0:T(4,128)} %param.5) | copy-start | bytes 18436

commit v4 on v3

--- a/solution.py
+++ b/solution.py
@@ -16,6 +16,7 @@
 ROWS = 512
 AHEAD = 2
 KDIM = 64
+WDIM = 48
 
 
 def split3(x):
@@ -52,8 +53,7 @@
     doubled = jnp.where(row < 4, pltpu.roll(x, 4, 0), x)
     first = doubled * jnp.where(row < 4, x[0:1], 1.0)
     second = doubled * jnp.where(row < 4, x[1:2], x[2:3])
-    zero = jnp.zeros_like(x)
-    return jnp.concatenate([*split3(first), *split3(second), zero, zero], axis=0).astype(jnp.bfloat16)
+    return jnp.concatenate([*split3(first), *split3(second)], axis=0).astype(jnp.bfloat16)
 
 
 def own_rows(x):
@@ -104,8 +104,8 @@
             tensor = jnp.where(i == j, 0.0, tensor)
         s_high, s_low = split2(scalar)
         t_high, t_low = split2(tensor)
-        acc_f[rows, :] += dot_nt(jnp.concatenate([s_high, s_low], axis=1), twice)
-        acc_h[rows, :] += dot_nt(jnp.concatenate([t_high, t_low], axis=1), twice)
+        acc_f[:, rows] += dot_nt(twice, jnp.concatenate([s_high, s_low], axis=1))
+        acc_h[:, rows] += dot_nt(twice, jnp.concatenate([t_high, t_low], axis=1))
         if far_f is not None:
             own = own_weights[:, rows]
             own = jnp.concatenate([own, own], axis=1)
@@ -134,7 +134,7 @@
     def behind(k):
         return lax.rem(me + n - k, n)
 
-    @pl.loop(1, n)
+    @pl.loop(1, n, unroll=n <= 16)
     def _(k):
         pl.semaphore_signal(barrier, inc=1, device_id={"tile": ahead(k)}, device_id_type=MESH)
 
@@ -151,6 +151,7 @@
     acc_f[...] = jnp.zeros_like(acc_f)
     acc_h[...] = jnp.zeros_like(acc_h)
 
+    pair_block(x, own_ref, own_w, acc_f, acc_h, None, None, True)
     pl.semaphore_wait(barrier, n - 1)
 
     def block_copy(k, slot):
@@ -175,8 +176,6 @@
     def _(k):
         block_copy(k, me).start()
 
-    pair_block(x, own_ref, own_w, acc_f, acc_h, None, None, True)
-
     @pl.loop(1, half)
     def _(k):
         @pl.when(k + AHEAD <= half)
@@ -198,7 +197,7 @@
         give_copy(half - 1).start()
     pair_block(gath[ahead(half)], own_ref, own_w, acc_f, acc_h, None, None, False)
 
-    image = combine(acc_f[...].T, acc_h[...].T, pos)
+    image = combine(acc_f[...], acc_h[...], pos)
 
     def added(k, running):
         give_copy(k).wait_recv()
@@ -215,7 +214,7 @@
         jnp.where(lane == 1, whole(force * image), jnp.where(lane == 2, whole(image * image), 0.0)),
     )
 
-    @pl.loop(1, n)
+    @pl.loop(1, n, unroll=n <= 16)
     def _(k):
         stat_copy(k, me).start()
 
@@ -227,7 +226,7 @@
     def _(k):
         give_copy(k).wait_send()
 
-    @pl.loop(1, n)
+    @pl.loop(1, n, unroll=n <= 16)
     def _(k):
         stat_copy(k, behind(k)).wait_recv()
 
@@ -239,7 +238,7 @@
     o_step[...] = jnp.broadcast_to(step, image.shape)
     o_ratio[...] = jnp.broadcast_to(new_norm / old_norm, image.shape)
 
-    @pl.loop(1, n)
+    @pl.loop(1, n, unroll=n <= 16)
     def _(k):
         stat_copy(k, me).wait_send()
 
@@ -259,11 +258,11 @@
             scratch_shapes=[
                 pltpu.VMEM((n, 8, size), jnp.float32),
                 pltpu.VMEM((size, KDIM), jnp.bfloat16),
-                pltpu.VMEM((KDIM, size), jnp.bfloat16),
-                pltpu.VMEM((size, KDIM), jnp.float32),
-                pltpu.VMEM((size, KDIM), jnp.float32),
-                pltpu.VMEM((KDIM, size), jnp.float32),
-                pltpu.VMEM((KDIM, size), jnp.float32),
+                pltpu.VMEM((WDIM, size), jnp.bfloat16),
+                pltpu.VMEM((WDIM, size), jnp.float32),
+                pltpu.VMEM((WDIM, size), jnp.float32),
+                pltpu.VMEM((WDIM, size), jnp.float32),
+                pltpu.VMEM((WDIM, size), jnp.float32),
                 pltpu.VMEM((n // 2, 3, size), jnp.float32),
                 pltpu.VMEM((n // 2, 3, size), jnp.float32),
                 pltpu.VMEM((n, 1, 128), jnp.float32),

time: 30.7 us -> 30.5 us (level)
  no operation moved by 1% of the time
where the time goes in v4:
time: 30.5 us; the launch traced here: 30.3 us
  Pallas kernels  28.2 us (92%)
  other arithmetic  1.34 us (4%)
  between operations  0.67 us (2%)
    pallas_call x1, Pallas kernels, shards(): pl.pallas_call(functools.partial(kernel, n), out_shape=(out, out, out), i...  28.2 us
    add x1, other arithmetic, shards(): new_residual + ratio * residual  1.34 us

profile of v4, /device:TPU:0, one launch (start us, length us, event | category | flops | bytes accessed | tf_op | source)
XLA Modules:
  0.0 30.3 jit_solution(16824344133194882210)
XLA Ops:
  0.6 0.0 copy-start
  0.6 0.0 copy-start.1
  0.7 28.2 %shard_map.58 = (f32[3,512]{1,0:T(4,128)}, f32[3,512]{1,0:T(4,128)}, f32[3,512]{1,0:T(4,128)}) custom-call(f32[3,512]{1,0:T(4,128)} %p_ref.1, f32[3,512]{1,0:T(4,128)} %f_ref.1), custom_call_target="tpu_custom_call" | custom-call | tf_op jit(solution)/shard_map/pallas_call | solution.py:253
  28.9 0.0 copy-done
  28.9 0.0 copy-done.1
  28.9 1.3 %multiply_add_fusion = (f32[3,512]{1,0:T(4,128)}, f32[3,512]{1,0:T(4,128)}, f32[3,512]{1,0:T(4,128)}) fusion(f32[3,512]{1,0:T(4,128)} %get-tuple-element.8, f32[3,512]{1,0:T(4,128)S(1)} %copy-done, f32[3,512]{1,0:T(4,128)} %get-tuple-element.6, f32[3,512]{1,0:T(4,128)} %get-tuple-element.7, f32[3,512]{1,0:T(4,128)S(1)} %copy-done.1), kind=kLoop, calls=%fused_computation | loop fusion | flops 9216 | bytes 49152 | tf_op jit(solution)/shard_map/add | solution.py:279
Async XLA Ops:
  0.6 28.3 %copy-start = (f32[3,512]{1,0:T(4,128)S(1)}, f32[3,512]{1,0:T(4,128)}, u32[]{:S(2)}) copy-start(f32[3,512]{1,0:T(4,128)} %f_ref.1) | copy-start | bytes 18436
  0.6 28.3 %copy-start.1 = (f32[3,512]{1,0:T(4,128)S(1)}, f32[3,512]{1,0:T(4,128)}, u32[]{:S(2)}) copy-start(f32[3,512]{1,0:T(4,128)} %param.5) | copy-start | bytes 18436
